TPU v7x, 32 devices: a whole 2x2x4 slice. The times are simulated.
32 devices in a mesh: dp: 16 (over z, x, core), seq: 2 (over y).
Axes of the slice: x: 2, y: 2, z: 4, core: 2. Of those that a mesh axis runs over, the one named last changes fastest.
Arguments:
- tokens: bfloat16 [16, 1152, 1024], P('dp', 'seq'), may hold values from -6 to 6
- w_qkv: bfloat16 [1024, 3072], P('dp'), may hold values from -0.1875 to 0.1875
- w_out: bfloat16 [1024, 1024], P('dp'), may hold values from -1 to 1
- w_up: bfloat16 [1024, 4096], P('dp'), may hold values from -0.1875 to 0.1875
- w_down: bfloat16 [4096, 1024], P('dp'), may hold values from -0.09375 to 0.09375
- gains: bfloat16 [1024, 2], P('dp'), may hold values from 0.5 to 1.5
- biases: bfloat16 [1024, 6], P('dp'), may hold values from -1.1953125 to 1.1953125
- up_bias: bfloat16 [4096], P('dp'), may hold values from -1.1953125 to 1.1953125
- valid: int32 [16], P('dp'), may hold values from 577 to 1152
- cotangent: bfloat16 [16, 1152, 1024], P('dp', 'seq'), may hold values from -6 to 6
Outputs:
- out_tokens: bfloat16 [16, 1152, 1024], P('dp', 'seq')
- grad_tokens: float32 [16, 1152, 1024], P('dp', 'seq')
- grad_qkv: float32 [1024, 3072], P('dp')
- grad_out: float32 [1024, 1024], P('dp')
- grad_up: float32 [1024, 4096], P('dp')
- grad_down: float32 [4096, 1024], P('dp')
- grad_gains: float32 [1024, 2], P('dp')
- grad_biases: float32 [1024, 6], P('dp')
- grad_up_bias: float32 [4096], P('dp')
Inputs may be any that keep to these rules, and one draw needn't show every extreme that they name: valid counts of the images; keys at positions from valid on are padding.
All inputs are finite; a program needn't handle non-finite values.
Results may differ from a plain program's by a relative error of at most 0.019.
Values may be sent and summed in bfloat16 or wider, within the bound.
A program may use at most 256 MiB of HBM per device.

v0:
```python
import jax
import jax.numpy as jnp
from jax import lax
from jax.sharding import PartitionSpec as P

HD = 64
EPSILON = 1e-06
NEG_FILL = -1e30


def layer_norm(values, scales, offset):
    average = jnp.mean(values, axis=-1, keepdims=True)
    centered = values - average
    variance = jnp.mean(centered * centered, axis=-1, keepdims=True)
    return centered * lax.rsqrt(variance + EPSILON) * scales + offset


def exact_gelu(values):
    return jax.nn.gelu(values, approximate=False)


def split_heads(block):
    seq_len = block.shape[0]
    return block.reshape(seq_len, block.shape[1] // HD, HD)


def score_block(query_heads, key_heads, length):
    scores = jnp.einsum("qhd,khd->hqk", query_heads, key_heads, preferred_element_type=jnp.float32)
    scores = scores * HD ** (-0.5)
    allowed = jnp.arange(key_heads.shape[0], dtype=jnp.int32) < length
    return jnp.where(allowed[None, None, :], scores, NEG_FILL)


def attend_forward(packed):
    queries, keyset, values, length = packed
    query_heads = split_heads(queries)
    key_heads = split_heads(keyset)
    value_heads = split_heads(values)
    scores = score_block(query_heads, key_heads, length)
    row_max = jnp.max(scores, axis=-1, keepdims=True)
    exp_scores = jnp.exp(scores - row_max)
    row_total = jnp.sum(exp_scores, axis=-1, keepdims=True)
    probs = (exp_scores / row_total).astype(jnp.bfloat16)
    result = jnp.einsum("hqk,khd->qhd", probs, value_heads, preferred_element_type=jnp.float32)
    log_total = row_max[..., 0] + jnp.log(row_total[..., 0])
    return (result.reshape(queries.shape).astype(jnp.bfloat16), log_total)


def attend_backward(packed):
    queries, keyset, values, length, log_total, grad_result = packed
    query_heads = split_heads(queries)
    key_heads = split_heads(keyset)
    value_heads = split_heads(values)
    grad_heads = split_heads(grad_result)
    scores = score_block(query_heads, key_heads, length)
    probs = jnp.exp(scores - log_total[:, :, None])
    grad_probs = jnp.einsum(
        "qhd,khd->hqk", grad_heads, value_heads, preferred_element_type=jnp.float32
    )
    row_delta = jnp.sum(probs * grad_probs, axis=-1, keepdims=True)
    grad_scores = (probs * (grad_probs - row_delta)).astype(jnp.bfloat16)
    grad_query = jnp.einsum(
        "hqk,khd->qhd", grad_scores, key_heads, preferred_element_type=jnp.float32
    ) * HD ** (-0.5)
    grad_key = jnp.einsum(
        "hqk,qhd->khd", grad_scores, query_heads, preferred_element_type=jnp.float32
    ) * HD ** (-0.5)
    grad_value = jnp.einsum(
        "hqk,qhd->khd", probs.astype(jnp.bfloat16), grad_heads, preferred_element_type=jnp.float32
    )
    flat_shape = queries.shape
    return (
        grad_query.reshape(flat_shape).astype(jnp.bfloat16),
        grad_key.reshape(flat_shape).astype(jnp.bfloat16),
        grad_value.reshape(flat_shape).astype(jnp.bfloat16),
    )


def per_device(tokens, w_qkv, w_out, w_up, w_down, gains, biases, up_bias, valid, cotangent):
    full_qkv, full_out, full_up, full_down, full_gains, full_biases, full_upb = (
        lax.all_gather(w_qkv, "dp", axis=0, tiled=True),
        lax.all_gather(w_out, "dp", axis=0, tiled=True),
        lax.all_gather(w_up, "dp", axis=0, tiled=True),
        lax.all_gather(w_down, "dp", axis=0, tiled=True),
        lax.all_gather(gains, "dp", axis=0, tiled=True),
        lax.all_gather(biases, "dp", axis=0, tiled=True),
        lax.all_gather(up_bias, "dp", axis=0, tiled=True),
    )
    gain_cols = full_gains.astype(jnp.float32)
    bias_cols = full_biases.astype(jnp.float32)
    upb_float = full_upb.astype(jnp.float32)
    images, local_len, model_width = tokens.shape
    token_shape = (images, local_len, model_width)
    flat_tokens = tokens.reshape(-1, model_width).astype(jnp.float32)
    normed_one, pull_one = jax.vjp(layer_norm, flat_tokens, gain_cols[:, 0], bias_cols[:, 0])
    first = normed_one.astype(jnp.bfloat16)
    mixed = jnp.dot(first, full_qkv, preferred_element_type=jnp.float32)
    queries = (mixed[:, :model_width] + bias_cols[:, 1]).astype(jnp.bfloat16)
    keyset = mixed[:, model_width : 2 * model_width].astype(jnp.bfloat16)
    values = (mixed[:, 2 * model_width :] + bias_cols[:, 2]).astype(jnp.bfloat16)
    head_q, head_k, head_v = (
        lax.all_to_all(
            queries.reshape(token_shape), "seq", split_axis=2, concat_axis=1, tiled=True
        ),
        lax.all_to_all(keyset.reshape(token_shape), "seq", split_axis=2, concat_axis=1, tiled=True),
        lax.all_to_all(values.reshape(token_shape), "seq", split_axis=2, concat_axis=1, tiled=True),
    )
    attended, log_totals = lax.map(attend_forward, (head_q, head_k, head_v, valid))
    back_tokens = lax.all_to_all(attended, "seq", split_axis=1, concat_axis=2, tiled=True)
    merged = back_tokens.reshape(-1, model_width)
    branch = jnp.dot(merged, full_out, preferred_element_type=jnp.float32) + bias_cols[:, 3]
    residual = flat_tokens + branch
    normed_two, pull_two = jax.vjp(layer_norm, residual, gain_cols[:, 1], bias_cols[:, 4])
    second = normed_two.astype(jnp.bfloat16)
    upward = jnp.dot(second, full_up, preferred_element_type=jnp.float32) + upb_float
    activated_float, pull_gelu = jax.vjp(exact_gelu, upward)
    activated = activated_float.astype(jnp.bfloat16)
    output = (
        residual
        + jnp.dot(activated, full_down, preferred_element_type=jnp.float32)
        + bias_cols[:, 5]
    )
    out_tokens = output.astype(jnp.bfloat16).reshape(token_shape)
    back_qkv, back_out, back_up, back_down = (full_qkv, full_out, full_up, full_down)
    grad_output = cotangent.reshape(-1, model_width)
    grad_down = jnp.dot(activated.T, grad_output, preferred_element_type=jnp.float32)
    grad_bias_down = jnp.sum(grad_output.astype(jnp.float32), axis=0)
    grad_act = jnp.dot(grad_output, back_down.T, preferred_element_type=jnp.float32)
    grad_upward = pull_gelu(grad_act)[0].astype(jnp.bfloat16)
    grad_up = jnp.dot(second.T, grad_upward, preferred_element_type=jnp.float32)
    grad_up_bias = jnp.sum(grad_upward.astype(jnp.float32), axis=0)
    grad_second = jnp.dot(grad_upward, back_up.T, preferred_element_type=jnp.float32)
    grad_resid_norm, grad_gain_two, grad_bias_two = pull_two(grad_second)
    grad_resid = grad_output.astype(jnp.float32) + grad_resid_norm
    grad_branch = grad_resid.astype(jnp.bfloat16)
    grad_out_weight = jnp.dot(merged.T, grad_branch, preferred_element_type=jnp.float32)
    grad_bias_out = jnp.sum(grad_branch.astype(jnp.float32), axis=0)
    grad_merged = jnp.dot(grad_branch, back_out.T, preferred_element_type=jnp.float32).astype(
        jnp.bfloat16
    )
    grad_head_result = lax.all_to_all(
        grad_merged.reshape(token_shape), "seq", split_axis=2, concat_axis=1, tiled=True
    )
    grad_q, grad_k, grad_v = lax.map(
        attend_backward, (head_q, head_k, head_v, valid, log_totals, grad_head_result)
    )
    tok_grad_q, tok_grad_k, tok_grad_v = (
        lax.all_to_all(grad_q, "seq", split_axis=1, concat_axis=2, tiled=True),
        lax.all_to_all(grad_k, "seq", split_axis=1, concat_axis=2, tiled=True),
        lax.all_to_all(grad_v, "seq", split_axis=1, concat_axis=2, tiled=True),
    )
    flat_grad_q = tok_grad_q.reshape(-1, model_width)
    flat_grad_v = tok_grad_v.reshape(-1, model_width)
    grad_mixed = jnp.concatenate(
        [flat_grad_q, tok_grad_k.reshape(-1, model_width), flat_grad_v], axis=1
    )
    grad_qkv = jnp.dot(first.T, grad_mixed, preferred_element_type=jnp.float32)
    grad_bias_q = jnp.sum(flat_grad_q.astype(jnp.float32), axis=0)
    grad_bias_v = jnp.sum(flat_grad_v.astype(jnp.float32), axis=0)
    grad_first = jnp.dot(grad_mixed, back_qkv.T, preferred_element_type=jnp.float32)
    grad_tok_norm, grad_gain_one, grad_bias_one = pull_one(grad_first)
    grad_tokens = (grad_resid + grad_tok_norm).reshape(token_shape)
    grad_gains = jnp.stack([grad_gain_one, grad_gain_two], axis=1)
    grad_biases = jnp.stack(
        [grad_bias_one, grad_bias_q, grad_bias_v, grad_bias_out, grad_bias_two, grad_bias_down],
        axis=1,
    )
    piece_qkv, piece_out, piece_up, piece_down, piece_gains, piece_biases, piece_upb = (
        lax.psum_scatter(
            grad_qkv.astype(jnp.bfloat16), "dp", scatter_dimension=0, tiled=True
        ).astype(jnp.float32),
        lax.psum_scatter(
            grad_out_weight.astype(jnp.bfloat16), "dp", scatter_dimension=0, tiled=True
        ).astype(jnp.float32),
        lax.psum_scatter(
            grad_up.astype(jnp.bfloat16), "dp", scatter_dimension=0, tiled=True
        ).astype(jnp.float32),
        lax.psum_scatter(
            grad_down.astype(jnp.bfloat16), "dp", scatter_dimension=0, tiled=True
        ).astype(jnp.float32),
        lax.psum_scatter(
            grad_gains.astype(jnp.bfloat16), "dp", scatter_dimension=0, tiled=True
        ).astype(jnp.float32),
        lax.psum_scatter(
            grad_biases.astype(jnp.bfloat16), "dp", scatter_dimension=0, tiled=True
        ).astype(jnp.float32),
        lax.psum_scatter(
            grad_up_bias.astype(jnp.bfloat16), "dp", scatter_dimension=0, tiled=True
        ).astype(jnp.float32),
    )
    totals = (
        lax.psum(piece_qkv.astype(jnp.bfloat16), "seq").astype(jnp.float32),
        lax.psum(piece_out.astype(jnp.bfloat16), "seq").astype(jnp.float32),
        lax.psum(piece_up.astype(jnp.bfloat16), "seq").astype(jnp.float32),
        lax.psum(piece_down.astype(jnp.bfloat16), "seq").astype(jnp.float32),
        lax.psum(piece_gains.astype(jnp.bfloat16), "seq").astype(jnp.float32),
        lax.psum(piece_biases.astype(jnp.bfloat16), "seq").astype(jnp.float32),
        lax.psum(piece_upb.astype(jnp.bfloat16), "seq").astype(jnp.float32),
    )
    return (
        out_tokens,
        grad_tokens,
        totals[0],
        totals[1],
        totals[2],
        totals[3],
        totals[4],
        totals[5],
        totals[6],
    )


def solution(mesh):
    return jax.shard_map(
        per_device,
        mesh=mesh,
        in_specs=(
            P("dp", "seq", None),
            P("dp", None),
            P("dp", None),
            P("dp", None),
            P("dp", None),
            P("dp", None),
            P("dp", None),
            P("dp"),
            P("dp"),
            P("dp", "seq", None),
        ),
        out_specs=(
            P("dp", "seq", None),
            P("dp", "seq", None),
            P("dp", None),
            P("dp", None),
            P("dp", None),
            P("dp", None),
            P("dp", None),
            P("dp", None),
            P("dp"),
        ),
        check_vma=False,
    )
```

profile of v0, /device:TPU:0, one launch (start us, length us, event | category | flops | bytes accessed | tf_op | source)
XLA Modules:
  0.0 1100.0 jit_solution(14046963542723650582)
XLA Ops:
  9.4 23.2 %all-gather = bf16[16,64,2]{1,2,0:T(2,128)(2,1)S(1)} all-gather(bf16[1,64,2]{1,2,0:T(2,128)(2,1)} %bitcast.251), channel_id=1, replica_groups=mesh['dp'=16,'seq'=2] {'dp'}, dimensions={0}, use_global_device_ids=true | all-gather | bytes 4352 | tf_op jit(solution)/shard_map/all_gather | solution.py:85
  32.7 17.9 %all-gather.1 = bf16[16,64,6]{1,2,0:T(8,128)(2,1)S(1)} all-gather(bf16[1,64,6]{1,2,0:T(8,128)(2,1)} %bitcast.250), channel_id=1, replica_groups=mesh['dp'=16,'seq'=2] {'dp'}, dimensions={0}, use_global_device_ids=true | all-gather | bytes 13056 | tf_op jit(solution)/shard_map/all_gather | solution.py:86
  53.4 21.5 %all-gather.8.cloned.1.call-done = bf16[1024,3072]{1,0:T(8,128)(2,1)} async-done(((bf16[64,3072]{1,0:T(8,128)(2,1)}), bf16[1024,3072]{1,0:T(8,128)(2,1)}) %all-gather.8.cloned.1.call-update) | async-done | bytes 6291472 | tf_op jit(solution)/shard_map/all_gather | solution.py:81
  208.8 16.1 %fusion.59 = (f32[8,1152]{1,0:T(8,128)S(1)}, f32[8,1152,1152]{1,2,0:T(8,128)}) fusion(bf16[1152,8,64]{0,2,1:T(8,128)(2,1)S(1)} %reshape.230, bf16[1152,8,64]{0,2,1:T(8,128)(2,1)S(1)} %reshape.232, pred[1152]{0:T(1024)(128)(4,1)S(1)} %iota_compare_fusion), kind=kOutput, calls=%fused_computation.104 | convolution fusion | flops 1390795776 | bytes 44864640 | tf_op jit(solution)/shard_map/while/body/eval_jaxpr/qhd,khd->hqk/dot_general | solution.py:28
  224.9 17.4 %fusion.1 = f32[8,1152]{1,0:T(8,128)S(1)} fusion(f32[8,1152,1152]{1,2,0:T(8,128)} %get-tuple-element.91, f32[8,1152]{1,0:T(8,128)S(1)} %get-tuple-element.90), kind=kLoop, calls=%fused_computation.7 | loop fusion | flops 21224448 | bytes 42541056 | tf_op jit(solution)/shard_map/while/body/eval_jaxpr/reduce_sum | solution.py:42
  242.4 18.1 %fusion.18 = bf16[8,64,1152]{2,1,0:T(8,128)(2,1)} fusion(bf16[1152,8,64]{0,2,1:T(8,128)(2,1)S(1)} %copy-done.17, f32[8,1152,1152]{1,2,0:T(8,128)} %get-tuple-element.91, f32[8,1152]{1,0:T(8,128)S(1)} %fusion.1, f32[8,1152]{1,0:T(8,128)S(1)} %get-tuple-element.90), kind=kOutput, calls=%fused_computation.39 | convolution fusion | flops 1391394816 | bytes 44900352 | tf_op jit(solution)/shard_map/while/body/eval_jaxpr/hqk,khd->qhd/dot_general | solution.py:44
  282.6 18.8 %all-gather.2 = bf16[16,1,256]{2,1,0:T(2,128)(2,1)S(1)} all-gather(bf16[1,1,256]{2,1,0:T(2,128)(2,1)S(1)} %reshape.246), channel_id=1, replica_groups=mesh['dp'=16,'seq'=2] {'dp'}, dimensions={0}, use_global_device_ids=true | all-gather | bytes 8704 | tf_op jit(solution)/shard_map/all_gather | solution.py:87
  310.8 30.8 %multiply_convert_fusion.1 = (bf16[576,4096]{1,0:T(8,128)(2,1)}, f32[576,4096]{1,0:T(8,128)}, f32[576,4096]{1,0:T(8,128)}) fusion(f32[4096]{0:T(1024)} %bitcast.240, bf16[1024,4096]{1,0:T(8,128)(2,1)} %all-gather.12.cloned.1.call-done, f32[576,1024]{1,0:T(8,128)S(1)} %get-tuple-element.93, f32[1024]{0:T(1024)} %bitcast.245, f32[1024]{0:T(1024)S(1)} %bitcast.234, ...), kind=kOutput, calls=%fused_computation.15 | convolution fusion | flops 4990500864 | bytes 34370048 | tf_op jit(solution)/shard_map/dot_general | solution.py:115
  341.7 15.7 %fusion.61 = (bf16[4096]{0:T(1024)(128)(2,1)}, bf16[576,4096]{1,0:T(8,128)(2,1)S(1)}) fusion(f32[576,4096]{1,0:T(8,128)} %get-tuple-element.79, bf16[4096,1024]{1,0:T(8,128)(2,1)} %all-gather.14.cloned.1.call-done, bf16[1,576,1024]{2,1,0:T(8,128)(2,1)S(1)} %copy-done.8, f32[576,4096]{1,0:T(8,128)} %get-tuple-element.94, f32[4096]{0:T(1024)} %bitcast.241), kind=kOutput, calls=%fused_computation.106 | convolution fusion | flops 4869582848 | bytes 33185792 | tf_op jit(solution)/shard_map/dot_general | solution.py:128
  357.4 10.7 multiply_reduce_fusion.1
  401.2 12.2 %all-to-all-done.4 = bf16[2,2,147456]{2,1,0:T(2,128)(2,1)} async-done(((bf16[2,2,147456]{2,1,0:T(2,128)(2,1)}), bf16[2,2,147456]{2,1,0:T(2,128)(2,1)}, u32[]{:S(2)}, u32[]{:S(2)}) %all-to-all-start.4) | async-done | bytes 1179680 | tf_op jit(solution)/shard_map/all_to_all | solution.py:141
  425.4 16.5 %fusion.15 = bf16[8,64,1152]{2,1,0:T(8,128)(2,1)S(1)} fusion(bf16[1152,8,64]{0,2,1:T(8,128)(2,1)S(1)} %reshape.237, f32[8,1152,1152]{1,2,0:T(8,128)} %get-tuple-element.91, f32[8,1152]{1,0:T(8,128)} %log_add_fusion), kind=kOutput, calls=%fused_computation.38 | convolution fusion | flops 1380777984 | bytes 44863488 | tf_op jit(solution)/shard_map/while/body/eval_jaxpr/hqk,qhd->khd/dot_general | solution.py:68
  442.0 32.1 %multiply_reduce_fusion = (f32[8,1152]{1,0:T(8,128)}, f32[8,1152,1152]{1,2,0:T(8,128)}) fusion(f32[8,1152,1152]{1,2,0:T(8,128)} %get-tuple-element.91, f32[8,1152]{1,0:T(8,128)} %log_add_fusion, bf16[1152,8,64]{0,2,1:T(8,128)(2,1)S(1)} %reshape.237, bf16[1152,8,64]{0,2,1:T(8,128)(2,1)S(1)} %copy-done.18), kind=kOutput, calls=%fused_computation.3 | convolution fusion | flops 1390795776 | bytes 87367680 | tf_op jit(solution)/shard_map/while/body/eval_jaxpr/qhd,khd->hqk/dot_general | solution.py:57
  492.1 34.8 %multiply_convert_fusion = bf16[8,1152,1152]{1,2,0:T(8,128)(2,1)} fusion(f32[8,1152,1152]{1,2,0:T(8,128)} %get-tuple-element.97, f32[8,1152,1152]{1,2,0:T(8,128)} %get-tuple-element.91, f32[8,1152]{1,0:T(8,128)S(1)} %copy-done.27, f32[8,1152]{1,0:T(8,128)S(1)} %copy-done.19), kind=kLoop, calls=%fused_computation.2 | loop fusion | flops 42467328 | bytes 106242048 | tf_op jit(solution)/shard_map/while/body/eval_jaxpr/convert_element_type | solution.py:61
  526.9 10.7 fusion.14
  555.7 10.5 fusion.13
  615.3 12.2 %convolution_convert_fusion = bf16[1024,4096]{1,0:T(8,128)(2,1)} fusion(bf16[576,4096]{1,0:T(8,128)(2,1)} %copy-done.49, f32[576,1024]{1,0:T(8,128)} %copy-done.10, f32[1024]{0:T(1024)} %bitcast.246, f32[1024]{0:T(1024)} %bitcast.237, f32[576]{0:T(1024)} %copy-done.40, f32[576]{0:T(1024)S(1)} %broadcast_multiply_fusion), kind=kOutput, calls=%fused_computation.29 | convolution fusion | flops 4838981632 | bytes 15479296 | tf_op jit(solution)/shard_map/dot_general | solution.py:130
  627.6 11.2 %convolution_convert_fusion.1 = bf16[4096,1024]{1,0:T(8,128)(2,1)} fusion(bf16[576,4096]{1,0:T(8,128)(2,1)} %get-tuple-element.78, bf16[1,576,1024]{2,1,0:T(8,128)(2,1)} %param.19), kind=kOutput, calls=%fused_computation.30 | convolution fusion | flops 4836032512 | bytes 14286848 | tf_op jit(solution)/shard_map/dot_general | solution.py:126
  664.7 31.7 %all-reduce = bf16[4096]{0:T(1024)(128)(2,1)S(1)} all-reduce(bf16[4096]{0:T(1024)(128)(2,1)} %get-tuple-element.99), channel_id=8, replica_groups=mesh['dp'=16,'seq'=2] {'dp'}, use_global_device_ids=true, to_apply=%region_32.33.clone | all-reduce | flops 4096 | bytes 16384
  698.9 107.8 %reduce-scatter.15.cloned.1.call-done = bf16[64,4096]{1,0:T(8,128)(2,1)} async-done(((bf16[1024,4096]{1,0:T(8,128)(2,1)}), bf16[64,4096]{1,0:T(8,128)(2,1)}) %reduce-scatter.15.cloned.1.call-update) | async-done | bytes 524304 | tf_op jit(solution)/shard_map/reduce_scatter | solution.py:175
  806.6 108.5 %reduce-scatter.17.cloned.1.call-done = bf16[256,1024]{1,0:T(8,128)(2,1)} async-done(((bf16[4096,1024]{1,0:T(8,128)(2,1)}), bf16[256,1024]{1,0:T(8,128)(2,1)}) %reduce-scatter.17.cloned.1.call-update) | async-done | bytes 524304 | tf_op jit(solution)/shard_map/reduce_scatter | solution.py:178
  927.9 46.4 %reduce-scatter.19.cloned.1.call-done = bf16[64,2]{1,0:T(8,128)(2,1)} async-done(((bf16[1024,2]{1,0:T(8,128)(2,1)}), bf16[64,2]{1,0:T(8,128)(2,1)}) %reduce-scatter.19.cloned.1.call-update) | async-done | bytes 272
  975.1 57.5 %reduce-scatter.21.cloned.1.call-done = bf16[64,6]{1,0:T(8,128)(2,1)} async-done(((bf16[1024,6]{1,0:T(8,128)(2,1)}), bf16[64,6]{1,0:T(8,128)(2,1)}) %reduce-scatter.21.cloned.1.call-update) | async-done | bytes 784
  1040.0 46.1 %all-reduce.5.cloned.1.call-done = (bf16[64,3072]{1,0:T(8,128)(2,1)}, bf16[64,1024]{1,0:T(8,128)(2,1)}, bf16[64,4096]{1,0:T(8,128)(2,1)}, bf16[256,1024]{1,0:T(8,128)(2,1)}) async-done(((bf16[64,3072]{1,0:T(8,128)(2,1)}, bf16[64,1024]{1,0:T(8,128)(2,1)}, bf16[64,4096]{1,0:T(8,128)(2,1)}, bf16[256,1024]{1,0:T(8,128)(2,1)}), (bf16[64,3072]{1,0:T(8,128)(2,1)}, bf16[64,1024]{1,0:T(8,128)(2,1)}, ...) | async-done | bytes 1572880 | tf_op jit(solution)/shard_map/psum | solution.py:192
  (267 shorter events, 355.1 us)
Async XLA Ops:
  7.2 45.0 %copy-start.2 = (bf16[1,576,1024]{2,1,0:T(8,128)(2,1)S(1)}, bf16[1,576,1024]{2,1,0:T(8,128)(2,1)}, u32[]{:S(2)}) copy-start(bf16[1,576,1024]{2,1,0:T(8,128)(2,1)} %param.10) | copy-start | bytes 3538948
  7.2 67.7 %all-gather.8.cloned.1.call-start = ((), (), s32[]{:S(2)}) async-start(), calls=%async_computation.14 | async-start | bytes 6684672 | tf_op jit(solution)/shard_map/all_gather | solution.py:81
  7.9 299.0 %all-gather.10.cloned.1.call-start = ((), (), s32[]{:S(2)}) async-start(), calls=%async_computation.15 | async-start | bytes 2228224 | tf_op jit(solution)/shard_map/all_gather | solution.py:82
  8.7 302.1 %all-gather.12.cloned.1.call-start = ((), (), s32[]{:S(2)}) async-start(), calls=%async_computation.16 | async-start | bytes 8912896 | tf_op jit(solution)/shard_map/all_gather | solution.py:83
  52.7 315.3 %copy-start.41 = (f32[1024,1]{0,1:T(1,128)}, f32[1024,1]{0,1:T(1,128)S(1)}, u32[]{:S(2)}) copy-start(f32[1024,1]{0,1:T(1,128)S(1)} %get-tuple-element.88) | copy-start | bytes 12292
  101.3 23.0 %all-to-all-start.1 = ((bf16[2,2,147456]{2,1,0:T(2,128)(2,1)}), bf16[2,2,147456]{2,1,0:T(2,128)(2,1)}, u32[]{:S(2)}, u32[]{:S(2)}) async-start(bf16[2,2,147456]{2,1,0:T(2,128)(2,1)} %reshape.262), calls=%async_computation.1 | async-start | bytes 2359296 | tf_op jit(solution)/shard_map/all_to_all | solution.py:102
  124.3 21.5 %all-to-all-start.2 = ((bf16[2,2,147456]{2,1,0:T(2,128)(2,1)}), bf16[2,2,147456]{2,1,0:T(2,128)(2,1)}, u32[]{:S(2)}, u32[]{:S(2)}) async-start(bf16[2,2,147456]{2,1,0:T(2,128)(2,1)} %reshape.264), calls=%async_computation.2 | async-start | bytes 2359296 | tf_op jit(solution)/shard_map/all_to_all | solution.py:105
  145.8 41.7 %all-to-all-start = ((bf16[2,2,147456]{2,1,0:T(2,128)(2,1)}), bf16[2,2,147456]{2,1,0:T(2,128)(2,1)}, u32[]{:S(2)}, u32[]{:S(2)}) async-start(bf16[2,2,147456]{2,1,0:T(2,128)(2,1)} %reshape.260), calls=%async_computation | async-start | bytes 2359296 | tf_op jit(solution)/shard_map/all_to_all | solution.py:106
  150.3 191.4 %all-gather.14.cloned.1.call-start = ((), (), s32[]{:S(2)}) async-start(), calls=%async_computation.17 | async-start | bytes 8912896 | tf_op jit(solution)/shard_map/all_gather | solution.py:84
  278.1 23.9 %all-to-all-start.3 = ((bf16[2,2,147456]{2,1,0:T(2,128)(2,1)}), bf16[2,2,147456]{2,1,0:T(2,128)(2,1)}, u32[]{:S(2)}, u32[]{:S(2)}) async-start(bf16[2,2,147456]{2,1,0:T(2,128)(2,1)} %reshape.266), calls=%async_computation.3 | async-start | bytes 2359296 | tf_op jit(solution)/shard_map/all_to_all | solution.py:109
  310.4 57.7 %copy-start.10 = (f32[576,1024]{1,0:T(8,128)}, f32[576,1024]{1,0:T(8,128)S(1)}, u32[]{:S(2)}) copy-start(f32[576,1024]{1,0:T(8,128)S(1)} %get-tuple-element.93) | copy-start | bytes 7077892
  310.8 57.3 %copy-start.40 = (f32[576]{0:T(1024)}, f32[576]{0:T(1024)S(1)}, u32[]{:S(2)}) copy-start(f32[576]{0:T(1024)S(1)} %fusion.46) | copy-start | bytes 6916
  392.8 20.6 %all-to-all-start.4 = ((bf16[2,2,147456]{2,1,0:T(2,128)(2,1)}), bf16[2,2,147456]{2,1,0:T(2,128)(2,1)}, u32[]{:S(2)}, u32[]{:S(2)}) async-start(bf16[2,2,147456]{2,1,0:T(2,128)(2,1)} %reshape.268), calls=%async_computation.4 | async-start | bytes 2359296 | tf_op jit(solution)/shard_map/all_to_all | solution.py:141
  397.3 299.1 %reduce-scatter.13.cloned.1.call-start = ((), (), s32[]{:S(2)}) async-start(), calls=%async_computation.19 | async-start | bytes 2228224 | tf_op jit(solution)/shard_map/reduce_scatter | solution.py:172
  487.6 63.7 %all-to-all-start.7 = ((bf16[2,2,147456]{2,1,0:T(2,128)(2,1)}), bf16[2,2,147456]{2,1,0:T(2,128)(2,1)}, u32[]{:S(2)}, u32[]{:S(2)}) async-start(bf16[2,2,147456]{2,1,0:T(2,128)(2,1)} %reshape.274), calls=%async_computation.7 | async-start | bytes 2359296 | tf_op jit(solution)/shard_map/all_to_all | solution.py:150
  551.2 28.5 %all-to-all-start.6 = ((bf16[2,2,147456]{2,1,0:T(2,128)(2,1)}), bf16[2,2,147456]{2,1,0:T(2,128)(2,1)}, u32[]{:S(2)}, u32[]{:S(2)}) async-start(bf16[2,2,147456]{2,1,0:T(2,128)(2,1)} %reshape.272), calls=%async_computation.6 | async-start | bytes 2359296 | tf_op jit(solution)/shard_map/all_to_all | solution.py:149
  579.8 19.1 %all-to-all-start.5 = ((bf16[2,2,147456]{2,1,0:T(2,128)(2,1)}), bf16[2,2,147456]{2,1,0:T(2,128)(2,1)S(1)}, u32[]{:S(2)}, u32[]{:S(2)}) async-start(bf16[2,2,147456]{2,1,0:T(2,128)(2,1)} %reshape.270), calls=%async_computation.5 | async-start | bytes 2359296 | tf_op jit(solution)/shard_map/all_to_all | solution.py:148
  583.4 115.5 %reduce-scatter.11.cloned.1.call-start = ((), (), s32[]{:S(2)}) async-start(), calls=%async_computation.18 | async-start | bytes 6684672 | tf_op jit(solution)/shard_map/reduce_scatter | solution.py:169
  615.3 191.4 %reduce-scatter.15.cloned.1.call-start = ((), (), s32[]{:S(2)}) async-start(), calls=%async_computation.20 | async-start | bytes 8912896 | tf_op jit(solution)/shard_map/reduce_scatter | solution.py:175
  627.5 287.6 %reduce-scatter.17.cloned.1.call-start = ((), (), s32[]{:S(2)}) async-start(), calls=%async_computation.21 | async-start | bytes 8912896 | tf_op jit(solution)/shard_map/reduce_scatter | solution.py:178
  638.8 335.5 %reduce-scatter.19.cloned.1.call-start = ((), (), s32[]{:S(2)}) async-start(), calls=%async_computation.22 | async-start | bytes 278528
  652.7 379.9 %reduce-scatter.21.cloned.1.call-start = ((), (), s32[]{:S(2)}) async-start(), calls=%async_computation.23 | async-start | bytes 278528
  659.5 255.7 %copy-start.43 = (f32[1024,1]{0,1:T(1,128)S(1)}, f32[1024,1]{0,1:T(1,128)}, u32[]{:S(2)}) copy-start(f32[1024,1]{0,1:T(1,128)} %get-tuple-element.82) | copy-start | bytes 12292
  662.7 423.5 %all-reduce.5.cloned.1.call-start = ((), (), s32[]{:S(2)}) async-start(), calls=%async_computation.24 | async-start | bytes 3145728 | tf_op jit(solution)/shard_map/psum | solution.py:192
  (45 other events, 507.2 us)
Sparse Core Ops, SparseCore 0:
  10.3 64.5 all-gather.7
  77.1 40.0 all-gather.9
  119.4 73.6 all-gather.11
  195.1 73.1 all-gather.13
  401.6 59.3 reduce-scatter.12
  615.4 83.4 reduce-scatter.10
  702.9 103.6 reduce-scatter.14
  810.7 104.3 reduce-scatter.16
  919.2 55.0 reduce-scatter.18
  978.2 54.3 reduce-scatter.20
  1035.1 51.0 all-reduce.4
where the time goes:
time: 1110 us; the launch traced here: 1100 us
  waiting for transfers between devices  405 us (36%)
  matrix products  226 us (20%)
  local copies, waits for them, and re-layouts  173 us (16%)
  other arithmetic  147 us (13%)
  blocking collectives  96.4 us (9%)
  starting transfers between devices  35.5 us (3%)
  between operations  16.6 us (1%)
    reduce_scatter x1, waiting for transfers between devices, per_device(): lax.psum_scatter(grad_down.astype(jnp.bfloat16), 'dp', scatter_dimension=...  108 us
    reduce_scatter x1, waiting for transfers between devices, per_device(): lax.psum_scatter(grad_up.astype(jnp.bfloat16), 'dp', scatter_dimension=0,...  108 us
    unnamed x13, waiting for transfers between devices  107 us
    unnamed x140, local copies, waits for them, and re-layouts  80.5 us
    unnamed x8, other arithmetic  71.4 us
    psum x1, waiting for transfers between devices, per_device(): lax.psum(piece_qkv.astype(jnp.bfloat16), 'seq').astype(jnp.float32)  46.1 us
    convert_element_type x1, other arithmetic, attend_backward(): grad_scores = (probs * (grad_probs - row_delta)).astype(jnp.bfloat16)  34.8 us
    dot_general x1, matrix products, attend_backward(): jnp.einsum('qhd,khd->hqk', grad_heads, value_heads, preferred_element_typ...  32.1 us
  transfers between devices with their start and end apart: 19, of which 8 were waited for; matrix products, arithmetic and copies ran while one was open for 44% of the time, Pallas kernels for 0%

commit v1 on v0

--- a/solution.py
+++ b/solution.py
@@ -1,3 +1,4 @@
+import functools
 import jax
 import jax.numpy as jnp
 from jax import lax
@@ -6,6 +7,22 @@
 HD = 64
 EPSILON = 1e-06
 NEG_FILL = -1e30
+
+
+def direct_bands(sample, peer_axis):
+    k_all = lax.axis_size(peer_axis)
+    frames = [(i0, (i0 + 1) % k_all) for i0 in range(k_all)]
+    xs_all = [(i0, (i0 - 1) % k_all) for i0 in range(k_all)]
+    near, main = ([sample], [sample])
+    for _ in range(k_all // 2):
+        near.append(lax.ppermute(near[-1], axis_name=peer_axis, perm=frames))
+    for _ in tuple(range((k_all - 1) // 2)):
+        main.append(lax.ppermute(main[-1], perm=xs_all, axis_name=peer_axis))
+    frame_out = jnp.concatenate([*near[::-1], *main[1:]], 0)
+    return jnp.roll(frame_out, (lax.axis_index(peer_axis) - k_all // 2) * sample.shape[0], 0)
+
+
+take_counts_on = functools.partial(direct_bands, peer_axis="dp")
 
 
 def layer_norm(values, scales, offset):
@@ -82,7 +99,7 @@
         lax.all_gather(w_out, "dp", axis=0, tiled=True),
         lax.all_gather(w_up, "dp", axis=0, tiled=True),
         lax.all_gather(w_down, "dp", axis=0, tiled=True),
-        lax.all_gather(gains, "dp", axis=0, tiled=True),
+        take_counts_on(gains),
         lax.all_gather(biases, "dp", axis=0, tiled=True),
         lax.all_gather(up_bias, "dp", axis=0, tiled=True),
     )

time: 1110 us -> 1110 us (level)
  starting transfers between devices: 35.5 us -> 68.8 us
  blocking collectives: 96.4 us -> 74.8 us
    ppermute x0 -> x15, starting transfers between devices: none -> 32.4 us  [the longest x7 31.3 us: direct_bands(): main.append(lax.ppermute(main[-1], perm=xs_all, axis_name=peer_axis))]
    all_gather x1 -> x0, blocking collectives: 23.2 us -> none  [per_device(): lax.all_gather(gains, 'dp', axis=0, tiled=True)]
    all_gather x1, waiting for transfers between devices: 21.5 us -> 0.02 us  [per_device(): lax.all_gather(w_qkv, 'dp', axis=0, tiled=True)]
    ppermute x0 -> x15, waiting for transfers between devices: none -> 13.4 us  [the longest x8 13.2 us: direct_bands(): near.append(lax.ppermute(near[-1], axis_name=peer_axis, perm=frames))]
    unnamed x140 -> x142, local copies, waits for them, and re-layouts: 80.5 us -> 80.4 us
  transfers between devices with their start and end apart: 19 -> 34, of which waited for: 8 -> 15; matrix products, arithmetic and copies ran while one was open for 44% -> 44% of each run, Pallas kernels for 0% -> 0%
where the time goes in v1:
time: 1110 us; the launch traced here: 1100 us
  waiting for transfers between devices  397 us (36%)
  matrix products  226 us (20%)
  local copies, waits for them, and re-layouts  173 us (16%)
  other arithmetic  147 us (13%)
  blocking collectives  74.8 us (7%)
  starting transfers between devices  68.8 us (6%)
  between operations  16.6 us (1%)
    reduce_scatter x1, waiting for transfers between devices, per_device(): lax.psum_scatter(grad_down.astype(jnp.bfloat16), 'dp', scatter_dimension=...  108 us
    reduce_scatter x1, waiting for transfers between devices, per_device(): lax.psum_scatter(grad_up.astype(jnp.bfloat16), 'dp', scatter_dimension=0,...  108 us
    unnamed x13, waiting for transfers between devices  106 us
    unnamed x142, local copies, waits for them, and re-layouts  80.4 us
    unnamed x8, other arithmetic  71.5 us
    psum x1, waiting for transfers between devices, per_device(): lax.psum(piece_qkv.astype(jnp.bfloat16), 'seq').astype(jnp.float32)  46.1 us
    convert_element_type x1, other arithmetic, attend_backward(): grad_scores = (probs * (grad_probs - row_delta)).astype(jnp.bfloat16)  34.7 us
    unnamed x1, blocking collectives  33 us
  transfers between devices with their start and end apart: 34, of which 15 were waited for; matrix products, arithmetic and copies ran while one was open for 44% of the time, Pallas kernels for 0%

profile of v1, /device:TPU:0, one launch (start us, length us, event | category | flops | bytes accessed | tf_op | source)
XLA Modules:
  0.0 1102.7 jit_solution(7542160958769585204)
XLA Ops:
  15.0 19.8 %all-gather = bf16[16,64,6]{1,2,0:T(8,128)(2,1)S(1)} all-gather(bf16[1,64,6]{1,2,0:T(8,128)(2,1)} %bitcast.247), channel_id=1, replica_groups=mesh['dp'=16,'seq'=2] {'dp'}, dimensions={0}, use_global_device_ids=true | all-gather | bytes 13056 | tf_op jit(solution)/shard_map/all_gather | solution.py:103
  212.0 16.8 %fusion.59 = (f32[8,1152]{1,0:T(8,128)S(1)}, f32[8,1152,1152]{1,2,0:T(8,128)}) fusion(bf16[1152,8,64]{0,2,1:T(8,128)(2,1)S(1)} %reshape.230, bf16[1152,8,64]{0,2,1:T(8,128)(2,1)S(1)} %reshape.232, pred[1152]{0:T(1024)(128)(4,1)S(1)} %iota_compare_fusion), kind=kOutput, calls=%fused_computation.104 | convolution fusion | flops 1390795776 | bytes 44864640 | tf_op jit(solution)/shard_map/while/body/eval_jaxpr/qhd,khd->hqk/dot_general | solution.py:45
  228.8 16.6 %fusion.1 = f32[8,1152]{1,0:T(8,128)S(1)} fusion(f32[8,1152,1152]{1,2,0:T(8,128)} %get-tuple-element.91, f32[8,1152]{1,0:T(8,128)S(1)} %get-tuple-element.90), kind=kLoop, calls=%fused_computation.7 | loop fusion | flops 21224448 | bytes 42541056 | tf_op jit(solution)/shard_map/while/body/eval_jaxpr/reduce_sum | solution.py:59
  245.4 18.1 %fusion.18 = bf16[8,64,1152]{2,1,0:T(8,128)(2,1)} fusion(bf16[1152,8,64]{0,2,1:T(8,128)(2,1)S(1)} %copy-done.17, f32[8,1152,1152]{1,2,0:T(8,128)} %get-tuple-element.91, f32[8,1152]{1,0:T(8,128)S(1)} %fusion.1, f32[8,1152]{1,0:T(8,128)S(1)} %get-tuple-element.90), kind=kOutput, calls=%fused_computation.39 | convolution fusion | flops 1391394816 | bytes 44900352 | tf_op jit(solution)/shard_map/while/body/eval_jaxpr/hqk,khd->qhd/dot_general | solution.py:61
  285.6 17.1 %all-gather.1 = bf16[16,1,256]{2,1,0:T(2,128)(2,1)S(1)} all-gather(bf16[1,1,256]{2,1,0:T(2,128)(2,1)S(1)} %reshape.244), channel_id=1, replica_groups=mesh['dp'=16,'seq'=2] {'dp'}, dimensions={0}, use_global_device_ids=true | all-gather | bytes 8704 | tf_op jit(solution)/shard_map/all_gather | solution.py:104
  312.3 30.8 %multiply_convert_fusion.1 = (bf16[576,4096]{1,0:T(8,128)(2,1)}, f32[576,4096]{1,0:T(8,128)}, f32[576,4096]{1,0:T(8,128)}) fusion(f32[4096]{0:T(1024)} %bitcast.237, bf16[1024,4096]{1,0:T(8,128)(2,1)} %all-gather.11.cloned.1.call-done, f32[576,1024]{1,0:T(8,128)S(1)} %get-tuple-element.93, f32[1024]{0:T(1024)} %bitcast.242, f32[1024]{0:T(1024)S(1)} %bitcast.231, ...), kind=kOutput, calls=%fused_computation.15 | convolution fusion | flops 4990500864 | bytes 34370048 | tf_op jit(solution)/shard_map/dot_general | solution.py:132
  343.1 15.7 %fusion.61 = (bf16[4096]{0:T(1024)(128)(2,1)}, bf16[576,4096]{1,0:T(8,128)(2,1)S(1)}) fusion(f32[576,4096]{1,0:T(8,128)} %get-tuple-element.79, bf16[4096,1024]{1,0:T(8,128)(2,1)} %all-gather.13.cloned.1.call-done, bf16[1,576,1024]{2,1,0:T(8,128)(2,1)S(1)} %copy-done.8, f32[576,4096]{1,0:T(8,128)} %get-tuple-element.94, f32[4096]{0:T(1024)} %bitcast.238), kind=kOutput, calls=%fused_computation.106 | convolution fusion | flops 4869582848 | bytes 33185792 | tf_op jit(solution)/shard_map/dot_general | solution.py:145
  358.8 10.7 multiply_reduce_fusion.1
  380.6 10.1 reduce.14
  402.8 12.2 %all-to-all-done.4 = bf16[2,2,147456]{2,1,0:T(2,128)(2,1)} async-done(((bf16[2,2,147456]{2,1,0:T(2,128)(2,1)}), bf16[2,2,147456]{2,1,0:T(2,128)(2,1)}, u32[]{:S(2)}, u32[]{:S(2)}) %all-to-all-start.4) | async-done | bytes 1179680 | tf_op jit(solution)/shard_map/all_to_all | solution.py:158
  427.0 16.5 %fusion.15 = bf16[8,64,1152]{2,1,0:T(8,128)(2,1)S(1)} fusion(bf16[1152,8,64]{0,2,1:T(8,128)(2,1)S(1)} %reshape.237, f32[8,1152,1152]{1,2,0:T(8,128)} %get-tuple-element.91, f32[8,1152]{1,0:T(8,128)} %log_add_fusion), kind=kOutput, calls=%fused_computation.38 | convolution fusion | flops 1380777984 | bytes 44863488 | tf_op jit(solution)/shard_map/while/body/eval_jaxpr/hqk,qhd->khd/dot_general | solution.py:85
  443.5 32.0 %multiply_reduce_fusion = (f32[8,1152]{1,0:T(8,128)}, f32[8,1152,1152]{1,2,0:T(8,128)}) fusion(f32[8,1152,1152]{1,2,0:T(8,128)} %get-tuple-element.91, f32[8,1152]{1,0:T(8,128)} %log_add_fusion, bf16[1152,8,64]{0,2,1:T(8,128)(2,1)S(1)} %reshape.237, bf16[1152,8,64]{0,2,1:T(8,128)(2,1)S(1)} %copy-done.18), kind=kOutput, calls=%fused_computation.3 | convolution fusion | flops 1390795776 | bytes 87367680 | tf_op jit(solution)/shard_map/while/body/eval_jaxpr/qhd,khd->hqk/dot_general | solution.py:74
  493.6 34.7 %multiply_convert_fusion = bf16[8,1152,1152]{1,2,0:T(8,128)(2,1)} fusion(f32[8,1152,1152]{1,2,0:T(8,128)} %get-tuple-element.97, f32[8,1152,1152]{1,2,0:T(8,128)} %get-tuple-element.91, f32[8,1152]{1,0:T(8,128)S(1)} %copy-done.27, f32[8,1152]{1,0:T(8,128)S(1)} %copy-done.19), kind=kLoop, calls=%fused_computation.2 | loop fusion | flops 42467328 | bytes 106242048 | tf_op jit(solution)/shard_map/while/body/eval_jaxpr/convert_element_type | solution.py:78
  528.3 10.7 fusion.14
  557.1 10.5 fusion.13
  616.6 12.2 %convolution_convert_fusion = bf16[1024,4096]{1,0:T(8,128)(2,1)} fusion(bf16[576,4096]{1,0:T(8,128)(2,1)} %copy-done.50, f32[576,1024]{1,0:T(8,128)} %copy-done.10, f32[1024]{0:T(1024)} %bitcast.243, f32[1024]{0:T(1024)} %bitcast.234, f32[576]{0:T(1024)} %copy-done.40, f32[576]{0:T(1024)S(1)} %broadcast_multiply_fusion), kind=kOutput, calls=%fused_computation.29 | convolution fusion | flops 4838981632 | bytes 15479296 | tf_op jit(solution)/shard_map/dot_general | solution.py:147
  628.9 11.1 %convolution_convert_fusion.1 = bf16[4096,1024]{1,0:T(8,128)(2,1)} fusion(bf16[576,4096]{1,0:T(8,128)(2,1)} %get-tuple-element.78, bf16[1,576,1024]{2,1,0:T(8,128)(2,1)} %param.19), kind=kOutput, calls=%fused_computation.30 | convolution fusion | flops 4836032512 | bytes 14286848 | tf_op jit(solution)/shard_map/dot_general | solution.py:143
  665.9 33.0 %all-reduce = bf16[4096]{0:T(1024)(128)(2,1)S(1)} all-reduce(bf16[4096]{0:T(1024)(128)(2,1)} %get-tuple-element.99), channel_id=8, replica_groups=mesh['dp'=16,'seq'=2] {'dp'}, use_global_device_ids=true, to_apply=%region_32.33.clone | all-reduce | flops 4096 | bytes 16384
  701.5 108.0 %reduce-scatter.15.cloned.1.call-done = bf16[64,4096]{1,0:T(8,128)(2,1)} async-done(((bf16[1024,4096]{1,0:T(8,128)(2,1)}), bf16[64,4096]{1,0:T(8,128)(2,1)}) %reduce-scatter.15.cloned.1.call-update) | async-done | bytes 524304 | tf_op jit(solution)/shard_map/reduce_scatter | solution.py:192
  809.5 108.4 %reduce-scatter.17.cloned.1.call-done = bf16[256,1024]{1,0:T(8,128)(2,1)} async-done(((bf16[4096,1024]{1,0:T(8,128)(2,1)}), bf16[256,1024]{1,0:T(8,128)(2,1)}) %reduce-scatter.17.cloned.1.call-update) | async-done | bytes 524304 | tf_op jit(solution)/shard_map/reduce_scatter | solution.py:195
  918.0 10.5 fusion.36
  930.7 46.4 %reduce-scatter.19.cloned.1.call-done = bf16[64,2]{1,0:T(8,128)(2,1)} async-done(((bf16[1024,2]{1,0:T(8,128)(2,1)}), bf16[64,2]{1,0:T(8,128)(2,1)}) %reduce-scatter.19.cloned.1.call-update) | async-done | bytes 272
  977.9 57.5 %reduce-scatter.21.cloned.1.call-done = bf16[64,6]{1,0:T(8,128)(2,1)} async-done(((bf16[1024,6]{1,0:T(8,128)(2,1)}), bf16[64,6]{1,0:T(8,128)(2,1)}) %reduce-scatter.21.cloned.1.call-update) | async-done | bytes 784
  1042.8 46.1 %all-reduce.5.cloned.1.call-done = (bf16[64,3072]{1,0:T(8,128)(2,1)}, bf16[64,1024]{1,0:T(8,128)(2,1)}, bf16[64,4096]{1,0:T(8,128)(2,1)}, bf16[256,1024]{1,0:T(8,128)(2,1)}) async-done(((bf16[64,3072]{1,0:T(8,128)(2,1)}, bf16[64,1024]{1,0:T(8,128)(2,1)}, bf16[64,4096]{1,0:T(8,128)(2,1)}, bf16[256,1024]{1,0:T(8,128)(2,1)}), (bf16[64,3072]{1,0:T(8,128)(2,1)}, bf16[64,1024]{1,0:T(8,128)(2,1)}, ...) | async-done | bytes 1572880 | tf_op jit(solution)/shard_map/psum | solution.py:209
  (298 shorter events, 380.6 us)
Async XLA Ops:
  7.2 70.7 %all-gather.7.cloned.1.call-start = ((), (), s32[]{:S(2)}) async-start(), calls=%async_computation.14 | async-start | bytes 6684672 | tf_op jit(solution)/shard_map/all_gather | solution.py:98
  7.9 300.4 %all-gather.9.cloned.1.call-start = ((), (), s32[]{:S(2)}) async-start(), calls=%async_computation.15 | async-start | bytes 2228224 | tf_op jit(solution)/shard_map/all_gather | solution.py:99
  8.7 303.6 %all-gather.11.cloned.1.call-start = ((), (), s32[]{:S(2)}) async-start(), calls=%async_computation.16 | async-start | bytes 8912896 | tf_op jit(solution)/shard_map/all_gather | solution.py:100
  9.4 28.0 %collective-permute-start = (bf16[64,2]{0,1:T(2,128)(2,1)}, bf16[64,2]{0,1:T(2,128)(2,1)S(1)}, u32[]{:S(2)}, u32[]{:S(2)}) collective-permute-start(bf16[64,2]{0,1:T(2,128)(2,1)} %param.15), channel_id=1, source_target_pairs={{0,2},{2,4},{4,6},{6,8},{8,10},{10,12},{12,14},{14,16},{16,18},{18... | collective-permute-start | bytes 776 | tf_op jit(solution)/shard_map/ppermute | solution.py:18
  9.9 27.9 %collective-permute-start.8 = (bf16[64,2]{0,1:T(2,128)(2,1)}, bf16[64,2]{0,1:T(2,128)(2,1)S(1)}, u32[]{:S(2)}, u32[]{:S(2)}) collective-permute-start(bf16[64,2]{0,1:T(2,128)(2,1)} %param.15), channel_id=1, source_target_pairs={{0,30},{2,0},{4,2},{6,4},{8,6},{10,8},{12,10},{14,12},{16,14},{18,... | collective-permute-start | bytes 776 | tf_op jit(solution)/shard_map/ppermute | solution.py:20
  43.1 5.8 collective-permute-start.2
  66.2 5.9 collective-permute-start.14
  71.8 5.9 collective-permute-start.7
  104.3 23.1 %all-to-all-start.1 = ((bf16[2,2,147456]{2,1,0:T(2,128)(2,1)}), bf16[2,2,147456]{2,1,0:T(2,128)(2,1)}, u32[]{:S(2)}, u32[]{:S(2)}) async-start(bf16[2,2,147456]{2,1,0:T(2,128)(2,1)} %reshape.259), calls=%async_computation.1 | async-start | bytes 2359296 | tf_op jit(solution)/shard_map/all_to_all | solution.py:119
  127.4 21.6 %all-to-all-start.2 = ((bf16[2,2,147456]{2,1,0:T(2,128)(2,1)}), bf16[2,2,147456]{2,1,0:T(2,128)(2,1)}, u32[]{:S(2)}, u32[]{:S(2)}) async-start(bf16[2,2,147456]{2,1,0:T(2,128)(2,1)} %reshape.261), calls=%async_computation.2 | async-start | bytes 2359296 | tf_op jit(solution)/shard_map/all_to_all | solution.py:122
  149.0 41.7 %all-to-all-start = ((bf16[2,2,147456]{2,1,0:T(2,128)(2,1)}), bf16[2,2,147456]{2,1,0:T(2,128)(2,1)}, u32[]{:S(2)}, u32[]{:S(2)}) async-start(bf16[2,2,147456]{2,1,0:T(2,128)(2,1)} %reshape.257), calls=%async_computation | async-start | bytes 2359296 | tf_op jit(solution)/shard_map/all_to_all | solution.py:123
  153.6 189.6 %all-gather.13.cloned.1.call-start = ((), (), s32[]{:S(2)}) async-start(), calls=%async_computation.17 | async-start | bytes 8912896 | tf_op jit(solution)/shard_map/all_gather | solution.py:101
  281.2 22.2 %all-to-all-start.3 = ((bf16[2,2,147456]{2,1,0:T(2,128)(2,1)}), bf16[2,2,147456]{2,1,0:T(2,128)(2,1)}, u32[]{:S(2)}, u32[]{:S(2)}) async-start(bf16[2,2,147456]{2,1,0:T(2,128)(2,1)} %reshape.263), calls=%async_computation.3 | async-start | bytes 2359296 | tf_op jit(solution)/shard_map/all_to_all | solution.py:126
  394.4 20.6 %all-to-all-start.4 = ((bf16[2,2,147456]{2,1,0:T(2,128)(2,1)}), bf16[2,2,147456]{2,1,0:T(2,128)(2,1)}, u32[]{:S(2)}, u32[]{:S(2)}) async-start(bf16[2,2,147456]{2,1,0:T(2,128)(2,1)} %reshape.265), calls=%async_computation.4 | async-start | bytes 2359296 | tf_op jit(solution)/shard_map/all_to_all | solution.py:158
  398.8 300.1 %reduce-scatter.13.cloned.1.call-start = ((), (), s32[]{:S(2)}) async-start(), calls=%async_computation.19 | async-start | bytes 2228224 | tf_op jit(solution)/shard_map/reduce_scatter | solution.py:189
  489.1 63.6 %all-to-all-start.7 = ((bf16[2,2,147456]{2,1,0:T(2,128)(2,1)}), bf16[2,2,147456]{2,1,0:T(2,128)(2,1)}, u32[]{:S(2)}, u32[]{:S(2)}) async-start(bf16[2,2,147456]{2,1,0:T(2,128)(2,1)} %reshape.271), calls=%async_computation.7 | async-start | bytes 2359296 | tf_op jit(solution)/shard_map/all_to_all | solution.py:167
  552.6 28.6 %all-to-all-start.6 = ((bf16[2,2,147456]{2,1,0:T(2,128)(2,1)}), bf16[2,2,147456]{2,1,0:T(2,128)(2,1)}, u32[]{:S(2)}, u32[]{:S(2)}) async-start(bf16[2,2,147456]{2,1,0:T(2,128)(2,1)} %reshape.269), calls=%async_computation.6 | async-start | bytes 2359296 | tf_op jit(solution)/shard_map/all_to_all | solution.py:166
  581.2 19.1 %all-to-all-start.5 = ((bf16[2,2,147456]{2,1,0:T(2,128)(2,1)}), bf16[2,2,147456]{2,1,0:T(2,128)(2,1)S(1)}, u32[]{:S(2)}, u32[]{:S(2)}) async-start(bf16[2,2,147456]{2,1,0:T(2,128)(2,1)} %reshape.267), calls=%async_computation.5 | async-start | bytes 2359296 | tf_op jit(solution)/shard_map/all_to_all | solution.py:165
  584.8 116.7 %reduce-scatter.11.cloned.1.call-start = ((), (), s32[]{:S(2)}) async-start(), calls=%async_computation.18 | async-start | bytes 6684672 | tf_op jit(solution)/shard_map/reduce_scatter | solution.py:186
  616.6 192.9 %reduce-scatter.15.cloned.1.call-start = ((), (), s32[]{:S(2)}) async-start(), calls=%async_computation.20 | async-start | bytes 8912896 | tf_op jit(solution)/shard_map/reduce_scatter | solution.py:192
  628.8 289.0 %reduce-scatter.17.cloned.1.call-start = ((), (), s32[]{:S(2)}) async-start(), calls=%async_computation.21 | async-start | bytes 8912896 | tf_op jit(solution)/shard_map/reduce_scatter | solution.py:195
  640.1 337.0 %reduce-scatter.19.cloned.1.call-start = ((), (), s32[]{:S(2)}) async-start(), calls=%async_computation.22 | async-start | bytes 278528
  654.0 381.3 %reduce-scatter.21.cloned.1.call-start = ((), (), s32[]{:S(2)}) async-start(), calls=%async_computation.23 | async-start | bytes 278528
  664.0 425.0 %all-reduce.5.cloned.1.call-start = ((), (), s32[]{:S(2)}) async-start(), calls=%async_computation.24 | async-start | bytes 3145728 | tf_op jit(solution)/shard_map/psum | solution.py:209
  (61 other events, 1380.0 us)
Sparse Core Ops, SparseCore 0:
  10.3 64.5 all-gather.6
  77.0 40.0 all-gather.8
  119.3 73.6 all-gather.10
  195.0 73.1 all-gather.12
  403.1 60.7 reduce-scatter.12
  616.7 84.7 reduce-scatter.10
  705.6 103.8 reduce-scatter.14
  813.5 104.3 reduce-scatter.16
  922.0 55.0 reduce-scatter.18
  981.0 54.2 reduce-scatter.20
  1037.8 51.0 all-reduce.4
